TPU v7x, 128 devices: a whole 4x4x4 slice. The times are simulated.
128 devices in a mesh: band: 16 (over x, y), grp: 8 (over z, core).
Axes of the slice: x: 4, y: 4, z: 4, core: 2. Of those that a mesh axis runs over, the one named last changes fastest.
Arguments:
- spectral: bfloat16 [640, 2, 4, 16, 640], P(('band', 'grp')), may hold values from -6 to 6
- legendre: bfloat16 [640, 640, 640], P(('band', 'grp')), may hold values from -4 to 4
- owner_table: int32 [640], replicated, may hold values from 0 to 639, as said below
Outputs:
- spectral_out: float32 [640, 2, 4, 16, 640], P(('band', 'grp'))
Inputs may be any that keep to these rules, and one draw needn't show every extreme that they name: `owner_table`: A permutation of the zonal wavenumbers. Slot s of the whole array belongs to device s // 5 along band+grp. For each q below 2, slots 2q and 2q + 1 of every device hold wavenumbers whose sum is (4q + 2) * 128 - 1.
All inputs are finite; a program needn't handle non-finite values.
Results may differ from a plain program's by a relative error of at most 0.0067.
Values may be sent and summed in bfloat16 or wider, within the bound.
A program may use at most 64 MiB of HBM per device.

v0:
```python
import math

import jax
import jax.numpy as jnp
from jax import lax
from jax.sharding import PartitionSpec as P

M = 640
NLAT = 1280
NLON = 2560
FIELDS = 4


def make_trig(wavenumber):
    lon_index = jnp.arange(NLON, dtype=jnp.int32)
    phases = wavenumber[:, None] * lon_index[None, :] % NLON
    angles = phases.astype(jnp.float32) * (2.0 * math.pi / NLON)
    return jnp.stack([jnp.cos(angles), -jnp.sin(angles)], axis=1).astype(jnp.bfloat16)


def on_device(spectral, legendre, owner_table):
    slot_count = spectral.shape[0]
    degrees = spectral.shape[-1]
    levels = spectral.shape[3]
    half_lat = legendre.shape[2]
    band_count = lax.axis_size("band")
    group_count = lax.axis_size("grp")
    device_count = band_count * group_count
    level_block = levels // band_count
    lat_block = NLAT // group_count
    row_total = 2 * FIELDS * levels
    row_width = FIELDS * level_block * lat_block
    slot_start = lax.axis_index(("band", "grp")) * slot_count
    wavenumber = lax.dynamic_slice_in_dim(owner_table, slot_start, slot_count)
    degree_index = jnp.arange(degrees, dtype=jnp.int32)
    keep_mask = (degree_index[None, :] >= wavenumber[:, None]).astype(jnp.bfloat16)
    odd_part = (degree_index[None, :] - wavenumber[:, None]) % 2
    flip_sign = (1 - 2 * odd_part).astype(jnp.bfloat16)
    spec_rows = spectral.reshape(slot_count, row_total, degrees) * keep_mask[:, None, :]
    both_rows = jnp.concatenate([spec_rows, spec_rows * flip_sign[:, None, :]], axis=1)
    halves = jnp.einsum("srn,snt->srt", both_rows, legendre, preferred_element_type=jnp.float32)
    northern = halves[:, :row_total]
    mirrored = halves[:, row_total:]
    fourier = jnp.concatenate([northern, jnp.flip(mirrored, axis=2)], axis=2)
    fourier = fourier.reshape(
        slot_count, 2, FIELDS, band_count, level_block, group_count, lat_block
    )
    fourier = jnp.transpose(fourier, (0, 1, 2, 3, 5, 4, 6))
    fourier_low = (fourier * (1.0 / math.sqrt(degrees))).astype(jnp.bfloat16)
    packed = fourier_low.reshape(1, slot_count, 2, FIELDS, device_count, level_block, lat_block)
    arrived = lax.all_to_all(packed, ("band", "grp"), split_axis=4, concat_axis=0, tiled=True)
    arrived = arrived.reshape(-1, 2, row_width)
    trig_rows = make_trig(owner_table)
    grid_values = jnp.einsum("scw,scl->wl", arrived, trig_rows, preferred_element_type=jnp.float32)
    grid_values = (grid_values * (1.0 / math.sqrt(M))).reshape(
        FIELDS, level_block * lat_block, NLON
    )
    product = (grid_values * jnp.roll(grid_values, -1, axis=0)).astype(jnp.bfloat16)
    zonal_coeffs = jnp.einsum(
        "wl,scl->scw",
        product.reshape(row_width, NLON),
        trig_rows,
        preferred_element_type=jnp.float32,
    )
    zonal_coeffs = (zonal_coeffs * (2.0 / math.sqrt(NLON))).astype(jnp.bfloat16)
    sendback = zonal_coeffs.reshape(device_count, slot_count, 2, FIELDS, 1, level_block, lat_block)
    returned = lax.all_to_all(sendback, ("band", "grp"), split_axis=0, concat_axis=4, tiled=True)
    returned = returned.reshape(
        slot_count, 2, FIELDS, band_count, group_count, level_block, lat_block
    )
    returned = jnp.transpose(returned, (0, 1, 2, 3, 5, 4, 6)).reshape(slot_count, row_total, NLAT)
    northern_part = returned[:, :, :half_lat].astype(jnp.float32)
    mirror_part = jnp.flip(returned[:, :, half_lat:], axis=2).astype(jnp.float32)
    plus_part = (northern_part + mirror_part).astype(jnp.bfloat16)
    minus_part = (northern_part - mirror_part).astype(jnp.bfloat16)
    stacked = jnp.concatenate([plus_part, minus_part], axis=1)
    projected = jnp.einsum("srt,snt->srn", stacked, legendre, preferred_element_type=jnp.float32)
    even_rows = flip_sign[:, None, :] > 0
    chosen = jnp.where(even_rows, projected[:, :row_total], projected[:, row_total:])
    chosen = chosen * keep_mask.astype(jnp.float32)[:, None, :] * (1.0 / math.sqrt(NLAT))
    return chosen.reshape(slot_count, 2, FIELDS, levels, degrees)


def solution(mesh):
    placed = (P(("band", "grp"), None, None, None, None), P(("band", "grp"), None, None), P())
    return jax.shard_map(
        on_device,
        mesh=mesh,
        in_specs=placed,
        out_specs=P(("band", "grp"), None, None, None, None),
        check_vma=False,
    )
```

profile of v0, /device:TPU:1, one launch (start us, length us, event | category | flops | bytes accessed | tf_op | source)
XLA Modules:
  0.0 157.3 jit_solution(6074803931011586506)
XLA Ops:
  0.0 0.8 dynamic_slice.3
  0.9 1.3 broadcast_multiply_fusion
  2.3 3.8 %fusion.15 = f32[5,256,640]{2,1,0:T(8,128)S(1)} fusion(bf16[5,640,640]{2,1,0:T(8,128)(2,1)} %param.4, bf16[5,128,640]{2,1,0:T(8,128)(2,1)S(1)} %get-tuple-element.5, bf16[5,128,640]{2,1,0:T(8,128)(2,1)S(1)} %get-tuple-element.6), kind=kOutput, calls=%fused_computation.27 | convolution fusion | flops 1051852800 | bytes 9011200 | tf_op jit(solution)/shard_map/srn,snt->srt/dot_general | solution.py:41
  6.3 9.3 %rev.8 = f32[5,128,640]{2,1,0:T(8,128)} reverse(f32[5,128,640]{2,1,0:T(8,128)S(1)} %get-tuple-element.8), dimensions={2} | reverse | bytes 3276800 | tf_op jit(solution)/shard_map/jit(_flip)/rev | solution.py:44
  15.6 2.9 %fusion.7 = bf16[5,128,1280]{2,1,0:T(8,128)(2,1)} fusion(f32[5,128,640]{2,1,0:T(8,128)} %rev.8, f32[5,128,640]{2,1,0:T(8,128)S(1)} %get-tuple-element.7), kind=kLoop, calls=%fused_computation.16 | loop fusion | flops 2457600 | bytes 4915200 | tf_op jit(solution)/shard_map/convert_element_type | solution.py:49
  18.5 4.5 %convert_element_type.80 = bf16[1,5,2,4,128,1,160]{6,4,3,2,1,5,0:T(8,128)(2,1)S(1)} reshape(bf16[5,128,1280]{2,1,0:T(8,128)(2,1)} %fusion.7) | data formatting | bytes 3276800 | tf_op jit(solution)/shard_map/convert_element_type | solution.py:49
  23.1 3.6 %copy.9 = bf16[1,5,2,4,128,1,160]{6,3,2,1,5,0,4:T(4,128)(2,1)} copy(bf16[1,5,2,4,128,1,160]{6,4,3,2,1,5,0:T(8,128)(2,1)S(1)} %convert_element_type.80) | data formatting | bytes 3276800 | tf_op jit(solution)/shard_map/convert_element_type | solution.py:49
  26.6 11.5 %all-to-all-start = ((bf16[1,5,2,4,128,1,160]{6,3,2,1,5,0,4:T(4,128)(2,1)}), bf16[1,5,2,4,128,1,160]{6,3,2,1,5,0,4:T(4,128)(2,1)S(1)}, u32[]{:S(2)}, u32[]{:S(2)}) async-start(bf16[1,5,2,4,128,1,160]{6,3,2,1,5,0,4:T(4,128)(2,1)} %copy.9), calls=%async_computation | async-start | bytes 5242880 | tf_op jit(solution)/shard_map/all_to_all | solution.py:51
  38.1 29.4 %cosine_convert_fusion = (bf16[640,1,2560]{2,0,1:T(8,128)(2,1)}, bf16[640,1,2560]{2,0,1:T(8,128)(2,1)}) fusion(s32[640]{0:T(1024)S(1)} %copy-done.2), kind=kLoop, calls=%fused_computation.9 | loop fusion | flops 19660800 | bytes 6556160 | tf_op jit(solution)/shard_map/convert
  67.6 6.6 %all-to-all-done = bf16[1,5,2,4,128,1,160]{6,3,2,1,5,0,4:T(4,128)(2,1)S(1)} async-done(((bf16[1,5,2,4,128,1,160]{6,3,2,1,5,0,4:T(4,128)(2,1)}), bf16[1,5,2,4,128,1,160]{6,3,2,1,5,0,4:T(4,128)(2,1)S(1)}, u32[]{:S(2)}, u32[]{:S(2)}) %all-to-all-start) | async-done | bytes 1638432 | tf_op jit(solution)/shard_map/all_to_all | solution.py:51
  74.2 4.5 %reshape.201 = bf16[640,2,640]{2,1,0:T(2,128)(2,1)} reshape(bf16[128,1,5,2,4,1,1,160]{7,4,3,2,0,6,5,1:T(4,128)(2,1)S(1)} %bitcast.35) | data formatting | bytes 3276800 | tf_op jit(solution)/shard_map/reshape | solution.py:52
  78.7 7.2 %bitcast_multiply_fusion.1 = f32[640,2560]{1,0:T(8,128)S(1)} fusion(bf16[640,1,2560]{2,0,1:T(8,128)(2,1)} %get-tuple-element.12, bf16[640,1,2560]{2,0,1:T(8,128)(2,1)} %get-tuple-element.11, bf16[640,2,640]{2,1,0:T(2,128)(2,1)} %reshape.201), kind=kOutput, calls=%fused_computation.7 | convolution fusion | flops 4199219200 | bytes 14745600 | tf_op jit(solution)/shard_map/scw,scl->wl/dot_general | solution.py:54
  86.4 0.4 pad_maximum_fusion.1
  86.8 3.3 %fusion.2 = bf16[640,2560]{1,0:T(8,128)(2,1)} fusion(f32[640,2560]{1,0:T(8,128)S(1)} %bitcast_multiply_fusion.1, f32[4,160,2560]{2,1,0:T(8,128)S(1)} %pad_maximum_fusion.1), kind=kLoop, calls=%fused_computation.6 | loop fusion | flops 3276800 | bytes 16384000 | tf_op jit(solution)/shard_map/convert_element_type | solution.py:58
  90.1 8.8 %multiply_convert_fusion = bf16[640,2,640]{2,0,1:T(8,128)(2,1)} fusion(bf16[640,2560]{1,0:T(8,128)(2,1)} %fusion.2, bf16[640,1,2560]{2,0,1:T(8,128)(2,1)} %get-tuple-element.12, bf16[640,1,2560]{2,0,1:T(8,128)(2,1)S(1)} %copy-done.1), kind=kOutput, calls=%fused_computation.18 | convolution fusion | flops 4199219200 | bytes 11468800 | tf_op jit(solution)/shard_map/wl,scl->scw/dot_general | solution.py:59
  98.9 3.5 %reshape.197 = bf16[128,5,2,4,1,1,160]{6,3,1,0,2,5,4:T(4,128)(2,1)S(1)} reshape(bf16[640,2,640]{2,0,1:T(8,128)(2,1)} %multiply_convert_fusion) | data formatting | bytes 3276800 | tf_op jit(solution)/shard_map/reshape | solution.py:66
  102.4 0.9 copy.12
  103.3 40.2 %all_to_all.30 = bf16[128,5,2,4,1,1,160]{6,3,1,2,5,4,0:T(4,128)(2,1)S(1)} all-to-all(bf16[128,5,2,4,1,1,160]{6,3,1,2,5,4,0:T(4,128)(2,1)S(1)} %copy.12), channel_id=1, replica_groups=mesh['band'=16,'grp'=8] {'band','grp'}, dimensions={0} | all-to-all | bytes 3276800 | tf_op jit(solution)/shard_map/all_to_all | solution.py:67
  143.5 0.6 copy.13
  144.2 3.6 %reshape_transpose_reshape.3 = bf16[5,128,1280]{2,1,0:T(8,128)(2,1)} reshape(bf16[1,5,2,4,128,1,1,160]{7,4,3,2,1,6,5,0:T(8,128)(2,1)S(1)} %copy.13) | data formatting | bytes 3276800 | tf_op jit(solution)/shard_map/reshape;transpose;reshape | solution.py:71
  147.8 1.3 slice.47
  149.1 2.6 %rev.9 = bf16[5,128,640]{2,1,0:T(8,128)(2,1)S(1)} reverse(bf16[5,128,640]{2,1,0:T(8,128)(2,1)S(1)} %slice.47), dimensions={2} | reverse | bytes 1638400 | tf_op jit(solution)/shard_map/jit(_flip)/rev | solution.py:73
  152.1 3.9 %fusion.19 = f32[5,256,640]{2,1,0:T(8,128)S(1)} fusion(bf16[5,640,640]{2,1,0:T(8,128)(2,1)} %param.4, bf16[5,128,640]{2,1,0:T(8,128)(2,1)S(1)} %get-tuple-element.10, bf16[5,128,640]{2,1,0:T(8,128)(2,1)S(1)} %get-tuple-element.9), kind=kOutput, calls=%fused_computation.31 | convolution fusion | flops 1051852800 | bytes 9011200 | tf_op jit(solution)/shard_map/srt,snt->srn/dot_general | solution.py:77
  156.0 1.4 fusion.14
  (12 shorter events, 1.2 us)
Async XLA Ops:
  26.6 11.5 %copy-start.2 = (s32[640]{0:T(1024)S(1)}, s32[640]{0:T(1024)}, u32[]{:S(2)}) copy-start(s32[640]{0:T(1024)} %param.5) | copy-start | bytes 7684
  26.6 47.6 %all-to-all-start = ((bf16[1,5,2,4,128,1,160]{6,3,2,1,5,0,4:T(4,128)(2,1)}), bf16[1,5,2,4,128,1,160]{6,3,2,1,5,0,4:T(4,128)(2,1)S(1)}, u32[]{:S(2)}, u32[]{:S(2)}) async-start(bf16[1,5,2,4,128,1,160]{6,3,2,1,5,0,4:T(4,128)(2,1)} %copy.9), calls=%async_computation | async-start | bytes 5242880 | tf_op jit(solution)/shard_map/all_to_all | solution.py:51
  86.8 3.3 %copy-start.1 = (bf16[640,1,2560]{2,0,1:T(8,128)(2,1)S(1)}, bf16[640,1,2560]{2,0,1:T(8,128)(2,1)}, u32[]{:S(2)}) copy-start(bf16[640,1,2560]{2,0,1:T(8,128)(2,1)} %get-tuple-element.11) | copy-start | bytes 9830404
  147.8 3.9 %copy-start = (bf16[5,128,1280]{2,1,0:T(8,128)(2,1)S(1)}, bf16[5,128,1280]{2,1,0:T(8,128)(2,1)}, u32[]{:S(2)}) copy-start(bf16[5,128,1280]{2,1,0:T(8,128)(2,1)} %reshape_transpose_reshape.3) | copy-start | bytes 4915204
where the time goes:
time: 158 us; the launch traced here: 157 us
  blocking collectives  40.2 us (25%)
  other arithmetic  39.2 us (25%)
  local copies, waits for them, and re-layouts  35.9 us (23%)
  matrix products  23.7 us (15%)
  starting transfers between devices  11.5 us (7%)
  waiting for transfers between devices  6.63 us (4%)
    all_to_all x1, blocking collectives, on_device(): lax.all_to_all(sendback, ('band', 'grp'), split_axis=0, concat_axis=4, ti...  40.2 us
    another operation x1, other arithmetic  29.4 us
    all_to_all x1, starting transfers between devices, on_device(): lax.all_to_all(packed, ('band', 'grp'), split_axis=4, concat_axis=0, tile...  11.5 us
    rev x1, local copies, waits for them, and re-layouts, on_device(): fourier = jnp.concatenate([northern, jnp.flip(mirrored, axis=2)], axis=2)  9.34 us
    dot_general x1, matrix products, on_device(): jnp.einsum('wl,scl->scw', product.reshape(row_width, NLON), trig_rows, pr...  8.82 us
    convert_element_type x2, local copies, waits for them, and re-layouts, on_device(): fourier_low = (fourier * (1.0 / math.sqrt(degrees))).astype(jnp.bfloat16)  8.09 us
    dot_general x1, matrix products, on_device(): jnp.einsum('scw,scl->wl', arrived, trig_rows, preferred_element_type=jnp....  7.23 us
    all_to_all x1, waiting for transfers between devices, on_device(): lax.all_to_all(packed, ('band', 'grp'), split_axis=4, concat_axis=0, tile...  6.63 us
  transfers between devices with their start and end apart: 1, of which 1 were waited for; matrix products, arithmetic and copies ran while one was open for 19% of the time, Pallas kernels for 0%

commit v1 on v0

v1 whole, which is shorter than its diff:
```python
import functools
import math

import jax
import jax.numpy as jnp
from jax import lax
from jax.experimental import pallas as pl
from jax.experimental.pallas import tpu as pltpu
from jax.sharding import PartitionSpec as P

M = 640
N = 640
NLAT = 1280
NLON = 2560
FIELDS = 4
LEV = 16
SLOTS = 5
BAND = 16
GRP = 8
DEV = BAND * GRP
ROWS = 2 * FIELDS * LEV
MESH = pl.DeviceIdType.MESH
F32 = jnp.float32
BF16 = jnp.bfloat16
GROUPS = ((0, 3), (3, 5))
NT = (((1,), (1,)), ((), ()))


def dot(a, b):
    return jnp.dot(a, b, preferred_element_type=F32)


def iota(shape, axis):
    return lax.broadcasted_iota(jnp.int32, shape, axis)


def turned_cos(turns, quarter):
    whole = jnp.floor(turns * (4.0 / NLON) + 0.5)
    x = (turns - whole * (NLON / 4.0)) * (2.0 * math.pi / NLON)
    y = x * x
    cosine = 1.0 + y * (-0.5 + y * (1.0 / 24 + y * (-1.0 / 720 + y * (1.0 / 40320))))
    sine = x * (1.0 + y * (-1.0 / 6 + y * (1.0 / 120 + y * (-1.0 / 5040 + y * (1.0 / 362880)))))
    k = whole + quarter
    k = k - 4.0 * jnp.floor(k * 0.25)
    odd = (k == 1.0) | (k == 3.0)
    value = jnp.where(odd, sine, cosine)
    return jnp.where((k == 1.0) | (k == 2.0), -value, value)


def pair_rows(x):
    return x.reshape(x.shape[0] // 2, 2, 128)


def flat_rows(x):
    return x.reshape(-1, 128)


def kernel(
    tab_smem, tab_ref, spec_hbm, leg_hbm, out_hbm,
    spec_v, leg_v, x_v, send_q, send_f, grid_q, grid_f, tt, tr, prod_q, prod_f,
    back_q, back_f, home_q, home_f, out_v,
    in_sem, out_sem, own_sem, ssem, rsem, plane_sem,
):
    b0 = lax.axis_index("band")
    g0 = lax.axis_index("grp")
    me = b0 * GRP + g0

    barrier = pltpu.get_barrier_semaphore()
    for i in range(1, BAND):
        pl.semaphore_signal(barrier, inc=1, device_id=((b0 + i) & (BAND - 1), g0), device_id_type=MESH)
    for i in range(1, GRP):
        pl.semaphore_signal(barrier, inc=1, device_id=(b0, (g0 + i) & (GRP - 1)), device_id_type=MESH)

    get_spec = pltpu.make_async_copy(spec_hbm, spec_v, in_sem.at[0])
    get_rem = pltpu.make_async_copy(leg_hbm.at[:, :, pl.ds(512, 128)], leg_v.at[:, :, pl.ds(512, 128)], in_sem.at[1])
    get_main = pltpu.make_async_copy(leg_hbm.at[:, :, pl.ds(0, 512)], leg_v.at[:, :, pl.ds(0, 512)], in_sem.at[2])
    get_spec.start()
    get_rem.start()
    get_main.start()

    degree = iota((1, N), 1)
    waves = [tab_smem[me * SLOTS + s] for s in range(SLOTS)]

    r = iota((ROWS, ROWS), 0)
    perm = jnp.where(iota((ROWS, ROWS), 1) == (r & 1) * 64 + (r >> 1), 1.0, 0.0).astype(BF16)
    get_spec.wait()
    for s in range(SLOTS):
        rows = dot(perm, spec_v[s])
        rows = jnp.where(degree >= waves[s], rows, 0.0)
        flip = jnp.where(((degree - waves[s]) & 1) == 1, -1.0, 1.0)
        x_v[s, :ROWS] = rows.astype(BF16)
        x_v[s, ROWS:] = (rows * flip).astype(BF16)

    pl.semaphore_wait(barrier, BAND - 1 + GRP - 1)
    for i in range(1, GRP):
        pl.semaphore_signal(plane_sem, inc=1, device_id=(b0, (g0 + i) & (GRP - 1)), device_id_type=MESH)

    scale_in = 1.0 / math.sqrt(N)
    lane_group = iota((32, 128), 1) >> 5
    get_rem.wait()
    for s in range(SLOTS):
        part = dot(x_v[s], leg_v[s, :, 512:640]) * scale_in
        for h in range(2):
            fields = [part[h * 128 + 32 * f : h * 128 + 32 * f + 32] for f in range(FIELDS)]
            for q in range(4):
                moved = [pltpu.roll(fields[f], (32 * (f - q)) % 128, 1) if f != q else fields[f] for f in range(FIELDS)]
                both = jnp.where(
                    lane_group < 2,
                    jnp.where(lane_group == 0, moved[0], moved[1]),
                    jnp.where(lane_group == 2, moved[2], moved[3]),
                )
                send_q[s, h * 4 + q] = pair_rows(both.astype(BF16))

    pl.semaphore_wait(plane_sem, GRP - 1)

    x0, y0, z0, c0 = b0 >> 2, b0 & 3, g0 >> 1, g0 & 1

    def peer(t):
        turn = t >> 1
        dx = turn & 3
        dy = ((turn >> 2) + turn) & 3
        dz = ((turn >> 4) + turn) & 3
        b = (((x0 + dx) & 3) << 2) + ((y0 + dy) & 3)
        g = (((z0 + dz) & 3) << 1) + ((c0 + t) & 1)
        return b, g

    def exchange(piece, source, target, which):
        def step(t, carry):
            b, g = peer(t)
            pltpu.make_async_remote_copy(
                src_ref=source(b, g), dst_ref=target, send_sem=ssem.at[which], recv_sem=rsem.at[which],
                device_id=(b, g), device_id_type=MESH,
            ).start()
            return carry

        lax.fori_loop(1, DEV, step, 0)
        own = pltpu.make_async_copy(source(b0, g0), target, own_sem.at[which])
        own.start()
        every = pltpu.make_async_remote_copy(
            src_ref=piece, dst_ref=piece, send_sem=ssem.at[which], recv_sem=rsem.at[which],
            device_id=(b0, g0), device_id_type=MESH,
        )
        return own, every

    def arrived(handle):
        handle[0].wait()
        handle[1].wait_recv()

    out_q = exchange(grid_q.at[:, pl.ds(0, DEV - 1)], lambda b, g: send_q.at[:, g, b], grid_q.at[:, me], 0)

    get_main.wait()

    def inverse(s, carry):
        part = dot(x_v[s], leg_v[s, :, 0:512]) * scale_in
        for h in range(2):
            for blk in range(4):
                piece = part[h * 128 : h * 128 + 128, blk * 128 : blk * 128 + 128].astype(BF16)
                send_f[s, h * 4 + blk] = piece.reshape(FIELDS, LEV, 2, 128)
        return carry

    lax.fori_loop(0, SLOTS, inverse, 0)
    out_f = exchange(grid_f.at[:, :, pl.ds(0, DEV - 1)], lambda b, g: send_f.at[:, g, :, b], grid_f.at[:, :, me], 1)

    tab = tab_ref[...].astype(F32)
    high = jnp.floor(tab * (1.0 / 32))
    low = tab - 32.0 * high
    row8 = iota((8, M), 0)
    split_rows = jnp.where(row8 == 0, high, jnp.where(row8 == 1, low, 0.0)).astype(BF16)
    high_rows = jnp.broadcast_to(high, (128, M)).astype(BF16)
    low_rows = jnp.broadcast_to(low, (128, M)).astype(BF16)

    def tables(s, carry):
        column = iota((M, 256), 0)
        pick = jnp.where(column == (iota((M, 256), 1) >> 1) * SLOTS + s, 1.0, 0.0).astype(BF16)
        found = dot(split_rows, pick)
        wave = found[0:1] * 32.0 + found[1:2]
        quarter = (iota((1, 256), 1) & 1).astype(F32)
        turn = 2.0 * turned_cos(wave * 128.0, 0.0)
        at = pl.multiple_of(s * 256, 256)

        def strip_tt(i, carry):
            line = (iota((32, 256), 0) + i * 32).astype(F32)
            last = turned_cos(wave * line, quarter)
            value = turned_cos(wave * (line + 128.0), quarter)
            tt[pl.ds(pl.multiple_of(i * 32, 32), 32), pl.ds(at, 256)] = last.astype(BF16)
            for a in range(1, NLON // 128):
                tt[pl.ds(pl.multiple_of(a * 128 + i * 32, 32), 32), pl.ds(at, 256)] = value.astype(BF16)
                value, last = turn * value - last, value
            return carry

        lax.fori_loop(0, 4, strip_tt, 0)

        lane = iota((256, M), 1)
        pick_rows = jnp.where(lane == (iota((256, M), 0) >> 1) * SLOTS + s, 1.0, 0.0).astype(BF16)
        wave_rows = 32.0 * lax.dot_general(pick_rows, high_rows, NT, preferred_element_type=F32)
        wave_rows = wave_rows + lax.dot_general(pick_rows, low_rows, NT, preferred_element_type=F32)
        for i in range(4):
            w = wave_rows[i * 64 : i * 64 + 64]
            line = iota((64, 128), 1).astype(F32)
            quarter = (iota((64, 128), 0) & 1).astype(F32)
            turn = 2.0 * turned_cos(w * 128.0, 0.0)
            last = turned_cos(w * line, quarter)
            value = turned_cos(w * (line + 128.0), quarter)
            tr[pl.ds(at + i * 64, 64), 0:128] = last.astype(BF16)
            for a in range(1, NLON // 128):
                tr[pl.ds(at + i * 64, 64), a * 128 : a * 128 + 128] = value.astype(BF16)
                value, last = turn * value - last, value
        return carry

    lax.fori_loop(0, SLOTS, tables, 0)

    scale_grid = 1.0 / math.sqrt(M)
    scale_zonal = 2.0 / math.sqrt(NLON)

    arrived(out_q)
    wide = jnp.concatenate([flat_rows(grid_q[s]) for s in range(SLOTS)], axis=0)

    def grid_quarter(i, carry):
        at = pl.ds(pl.multiple_of(i * 512, 512), 512)
        values = dot(tt[at, :], wide) * scale_grid
        prod_q[at, :] = (values * pltpu.roll(values, 96, 1)).astype(BF16)
        return carry

    lax.fori_loop(0, NLON // 512, grid_quarter, 0)

    def zonal_quarter(s, carry):
        values = dot(tr[pl.ds(pl.multiple_of(s * 256, 256), 256), :], prod_q[...]) * scale_zonal
        back_q[s] = pair_rows(values.astype(BF16))
        return carry

    lax.fori_loop(0, SLOTS, zonal_quarter, 0)

    arrived(out_f)
    ret_q = exchange(back_q.at[:, pl.ds(0, DEV - 1)], lambda b, g: back_q.at[:, b * GRP + g], home_q.at[:, g0, b0], 2)

    wide = jnp.concatenate(
        [jnp.concatenate([flat_rows(grid_f[s, f]) for s in range(SLOTS)], axis=0) for f in range(FIELDS)], axis=1
    )

    def grid_full(i, carry):
        at = pl.ds(pl.multiple_of(i * 256, 256), 256)
        values = dot(tt[at, :], wide) * scale_grid
        following = jnp.concatenate([values[:, 128:], values[:, :128]], axis=1)
        prod_f[at, :] = (values * following).astype(BF16)
        return carry

    lax.fori_loop(0, NLON // 256, grid_full, 0)

    def zonal_full(s, carry):
        values = dot(tr[pl.ds(pl.multiple_of(s * 256, 256), 256), :], prod_f[...]) * scale_zonal
        for f in range(FIELDS):
            back_f[s, f] = pair_rows(values[:, f * 128 : f * 128 + 128].astype(BF16))
        return carry

    returns = []
    for i, (lo, hi) in enumerate(GROUPS):
        lax.fori_loop(lo, hi, zonal_full, 0)
        span = pl.ds(lo, hi - lo)
        returns.append(
            exchange(
                back_f.at[span, :, pl.ds(0, DEV - 1)],
                lambda b, g, span=span: back_f.at[span, :, b * GRP + g],
                home_f.at[span, g0, :, b0],
                3 + i,
            )
        )

    r = iota((2 * ROWS, 2 * ROWS), 0)
    j = iota((2 * ROWS, 2 * ROWS), 1)
    hit = (j & 127) == ((r & 63) << 1) + ((r >> 6) & 1)
    both_signs = jnp.where(hit, jnp.where((r >= ROWS) & (j >= ROWS), -1.0, 1.0), 0.0).astype(BF16)
    scale_out = 1.0 / math.sqrt(NLAT)

    def direct(s):
        halves = []
        for h in range(2):
            parts = [flat_rows(home_f[s, h * 4 + blk]) for blk in range(4)]
            quarters = [flat_rows(home_q[s, h * 4 + q]).astype(F32) for q in range(4)]
            mixed = []
            for f in range(FIELDS):
                moved = [pltpu.roll(quarters[q], (32 * (q - f)) % 128, 1) if q != f else quarters[q] for q in range(4)]
                mixed.append(
                    jnp.where(
                        lane_group < 2,
                        jnp.where(lane_group == 0, moved[0], moved[1]),
                        jnp.where(lane_group == 2, moved[2], moved[3]),
                    )
                )
            parts.append(jnp.concatenate(mixed, axis=0).astype(BF16))
            halves.append(jnp.concatenate(parts, axis=1))
        folded = dot(both_signs, jnp.concatenate(halves, axis=0)).astype(BF16)
        result = lax.dot_general(folded, leg_v[s], NT, preferred_element_type=F32)
        chosen = jnp.where(((degree - waves[s]) & 1) == 0, result[:ROWS], result[ROWS:])
        out_v[s] = jnp.where(degree >= waves[s], chosen * scale_out, 0.0)

    arrived(ret_q)
    puts = []
    for i, (lo, hi) in enumerate(GROUPS):
        arrived(returns[i])
        for s in range(lo, hi):
            direct(s)
            puts.append(pltpu.make_async_copy(out_v.at[s], out_hbm.at[s], out_sem.at[s]))
            puts[-1].start()
    for handle in [out_q, out_f, ret_q] + returns:
        handle[1].wait_send()
    for put in puts:
        put.wait()


def on_device(spectral, legendre, owner_table):
    anywhere = pl.BlockSpec(memory_space=pl.ANY)
    out = pl.pallas_call(
        kernel,
        out_shape=jax.ShapeDtypeStruct((SLOTS, ROWS, N), F32),
        in_specs=[
            pl.BlockSpec(memory_space=pltpu.SMEM),
            pl.BlockSpec(memory_space=pltpu.VMEM),
            anywhere,
            anywhere,
        ],
        out_specs=anywhere,
        scratch_shapes=[
            pltpu.VMEM((SLOTS, ROWS, N), BF16),
            pltpu.VMEM((SLOTS, N, N), BF16),
            pltpu.VMEM((SLOTS, 2 * ROWS, N), BF16),
            pltpu.VMEM((SLOTS, GRP, LEV, 2, 128), BF16),
            pltpu.VMEM((SLOTS, GRP, FIELDS, LEV, 2, 128), BF16),
            pltpu.VMEM((SLOTS, DEV, 2, 128), BF16),
            pltpu.VMEM((SLOTS, FIELDS, DEV, 2, 128), BF16),
            pltpu.VMEM((NLON, 2 * M), BF16),
            pltpu.VMEM((2 * M, NLON), BF16),
            pltpu.VMEM((NLON, 128), BF16),
            pltpu.VMEM((NLON, 512), BF16),
            pltpu.VMEM((SLOTS, DEV, 2, 128), BF16),
            pltpu.VMEM((SLOTS, FIELDS, DEV, 2, 128), BF16),
            pltpu.VMEM((SLOTS, GRP, LEV, 2, 128), BF16),
            pltpu.VMEM((SLOTS, GRP, FIELDS, LEV, 2, 128), BF16),
            pltpu.VMEM((SLOTS, ROWS, N), F32),
            pltpu.SemaphoreType.DMA((3,)),
            pltpu.SemaphoreType.DMA((SLOTS,)),
            pltpu.SemaphoreType.DMA((3 + len(GROUPS),)),
            pltpu.SemaphoreType.DMA((3 + len(GROUPS),)),
            pltpu.SemaphoreType.DMA((3 + len(GROUPS),)),
            pltpu.SemaphoreType.REGULAR,
        ],
        compiler_params=pltpu.CompilerParams(
            collective_id=0, has_side_effects=True, vmem_limit_bytes=60 << 20
        ),
    )(
        owner_table,
        owner_table.reshape(1, M),
        spectral.reshape(SLOTS, ROWS, N),
        legendre,
    )
    return out.reshape(SLOTS, 2, FIELDS, LEV, N)


def solution(mesh):
    placed = (P(("band", "grp"), None, None, None, None), P(("band", "grp"), None, None), P())
    return jax.shard_map(
        on_device,
        mesh=mesh,
        in_specs=placed,
        out_specs=P(("band", "grp"), None, None, None, None),
        check_vma=False,
    )
```

time: 158 us -> 69.7 us (0.44)
  Pallas kernels: 0 us -> 65.5 us
  blocking collectives: 40.2 us -> 0 us
  other arithmetic: 39.2 us -> 0 us
  local copies, waits for them, and re-layouts: 35.9 us -> 4 us
  matrix products: 23.7 us -> 0 us
  starting transfers between devices: 11.5 us -> 0 us
  waiting for transfers between devices: 6.63 us -> 0 us
    pallas_call x0 -> x1, Pallas kernels: none -> 65.5 us  [on_device(): pl.pallas_call(kernel, out_shape=jax.ShapeDtypeStruct((SLOTS, ROWS, N), F...]
    all_to_all x1 -> x0, blocking collectives: 40.2 us -> none  [on_device(): lax.all_to_all(sendback, ('band', 'grp'), split_axis=0, concat_axis=4, ti...]
    another operation x1 -> x0, other arithmetic: 29.4 us -> none
    dot_general x4 -> x0, matrix products: 23.7 us -> none  [the longest x1 8.82 us: on_device(): jnp.einsum('wl,scl->scw', product.reshape(row_width, NLON), trig_rows, pr...]
    rev x2 -> x0, local copies, waits for them, and re-layouts: 11.9 us -> none  [the longest x1 9.34 us: on_device(): fourier = jnp.concatenate([northern, jnp.flip(mirrored, axis=2)], axis=2)]
    all_to_all x1 -> x0, starting transfers between devices: 11.5 us -> none  [on_device(): lax.all_to_all(packed, ('band', 'grp'), split_axis=4, concat_axis=0, tile...]
    convert_element_type x2 -> x0, local copies, waits for them, and re-layouts: 8.09 us -> none  [on_device(): fourier_low = (fourier * (1.0 / math.sqrt(degrees))).astype(jnp.bfloat16)]
    reshape x3 -> x1, local copies, waits for them, and re-layouts: 8.91 us -> 1.27 us  [on_device(): owner_table.reshape(1, M)]
  transfers between devices with their start and end apart: 1 -> 0, of which waited for: 1 -> 0; matrix products, arithmetic and copies ran while one was open for 19% -> 0% of each run, Pallas kernels for 0% -> 0%
where the time goes in v1:
time: 69.7 us; the launch traced here: 69.5 us
  Pallas kernels  65.5 us (94%)
  local copies, waits for them, and re-layouts  4 us (6%)
    pallas_call x1, Pallas kernels, on_device(): pl.pallas_call(kernel, out_shape=jax.ShapeDtypeStruct((SLOTS, ROWS, N), F...  65.5 us
    unnamed x1, local copies, waits for them, and re-layouts  2.73 us

profile of v1, /device:TPU:1, one launch (start us, length us, event | category | flops | bytes accessed | tf_op | source)
XLA Modules:
  0.0 69.5 jit_solution(8923981368578638283)
XLA Ops:
  0.0 1.3 %reshape.9.tab_ref = s32[1,640]{1,0:T(1,128)} reshape(s32[640]{0:T(1024)} %tab_smem.1) | data formatting | bytes 5120 | tf_op jit(solution)/shard_map/reshape | solution.py:351
  1.3 65.5 %shard_map.37 = f32[5,128,640]{2,1,0:T(8,128)} custom-call(s32[640]{0:T(1024)} %tab_smem.1, s32[1,640]{1,0:T(1,128)} %reshape.9.tab_ref, bf16[5,128,640]{2,1,0:T(8,128)(2,1)} %bitcast.3, bf16[5,640,640]{2,1,0:T(8,128)(2,1)} %leg_hbm.1), custom_call_target="tpu_custom_call" | custom-call | tf_op jit(solution)/shard_map/pallas_call | solution.py:312
  66.8 2.7 %copy.5 = f32[5,2,4,16,640]{4,3,2,1,0:T(8,128)} copy(f32[5,2,4,16,640]{4,3,2,1,0:T(8,128)} %bitcast.2) | data formatting | bytes 3276800

commit v2 on v1

v2 whole, which is shorter than its diff:
```python
import functools
import math

import jax
import jax.numpy as jnp
from jax import lax
from jax.experimental import pallas as pl
from jax.experimental.pallas import tpu as pltpu
from jax.sharding import PartitionSpec as P

M = 640
N = 640
NLAT = 1280
NLON = 2560
FIELDS = 4
LEV = 16
SLOTS = 5
BAND = 16
GRP = 8
DEV = BAND * GRP
ROWS = 2 * FIELDS * LEV
MESH = pl.DeviceIdType.MESH
F32 = jnp.float32
BF16 = jnp.bfloat16
RETURNS = ((0, 2), (2, 4), (4, 5))
HALF = NLON // 2
PART = 3 * 2 * DEV
NT = (((1,), (1,)), ((), ()))


def dot(a, b):
    return jnp.dot(a, b, preferred_element_type=F32)


def iota(shape, axis):
    return lax.broadcasted_iota(jnp.int32, shape, axis)


def turned_cos(turns, quarter):
    whole = jnp.floor(turns * (4.0 / NLON) + 0.5)
    x = (turns - whole * (NLON / 4.0)) * (2.0 * math.pi / NLON)
    y = x * x
    cosine = 1.0 + y * (-0.5 + y * (1.0 / 24 + y * (-1.0 / 720 + y * (1.0 / 40320))))
    sine = x * (1.0 + y * (-1.0 / 6 + y * (1.0 / 120 + y * (-1.0 / 5040 + y * (1.0 / 362880)))))
    k = whole + quarter
    k = k - 4.0 * jnp.floor(k * 0.25)
    odd = (k == 1.0) | (k == 3.0)
    value = jnp.where(odd, sine, cosine)
    return jnp.where((k == 1.0) | (k == 2.0), -value, value)


def pair_rows(x):
    return x.reshape(x.shape[0] // 2, 2, 128)


def flat_rows(x):
    return x.reshape(-1, 128)


def swap_halves(first, second, low):
    a, b = pltpu.roll(first, 64, 1), pltpu.roll(second, 64, 1)
    return jnp.where(low, a, b), jnp.where(low, b, a)


def pick_group(lane_group, x):
    return jnp.where(
        lane_group < 2,
        jnp.where(lane_group == 0, x[0], x[1]),
        jnp.where(lane_group == 2, x[2], x[3]),
    )


def kernel(
    tab_smem, tab_ref, spec_hbm, leg_hbm, out_v,
    spec_v, leg_v, x_v, send_a, send_b, grid_a, grid_b, tt, tr, tr4, prod_a, prod_b,
    back_a, back_b, home_a, home_b,
    in_sem, own_sem, ssem, rsem, plane_sem,
):
    b0 = lax.axis_index("band")
    g0 = lax.axis_index("grp")
    me = b0 * GRP + g0

    barrier = pltpu.get_barrier_semaphore()
    for i in range(1, BAND):
        pl.semaphore_signal(barrier, inc=1, device_id=((b0 + i) & (BAND - 1), g0), device_id_type=MESH)
    for i in range(1, GRP):
        pl.semaphore_signal(barrier, inc=1, device_id=(b0, (g0 + i) & (GRP - 1)), device_id_type=MESH)

    cols_a, cols_b = pl.ds(0, 256), pl.ds(256, 384)
    get_spec = pltpu.make_async_copy(spec_hbm, spec_v, in_sem.at[0])
    get_a = pltpu.make_async_copy(leg_hbm.at[:, :, cols_a], leg_v.at[:, :, cols_a], in_sem.at[1])
    get_b = pltpu.make_async_copy(leg_hbm.at[:, :, cols_b], leg_v.at[:, :, cols_b], in_sem.at[2])
    get_spec.start()
    get_a.start()
    get_b.start()

    degree = iota((1, N), 1)
    waves = [tab_smem[me * SLOTS + s] for s in range(SLOTS)]
    ordered = [(waves[2 * p] & 1) == 0 for p in range(2)]

    def sorted_pairs(x):
        pairs = []
        for p in range(2):
            pairs.append(jnp.where(ordered[p], x[2 * p], x[2 * p + 1]))
            pairs.append(jnp.where(ordered[p], x[2 * p + 1], x[2 * p]))
        return pairs + [x[4]]

    r = iota((ROWS, ROWS), 0)
    perm = jnp.where(iota((ROWS, ROWS), 1) == (r & 1) * 64 + (r >> 1), 1.0, 0.0).astype(BF16)
    get_spec.wait()
    for s in range(SLOTS):
        rows = dot(perm, spec_v[s])
        rows = jnp.where(degree >= waves[s], rows, 0.0)
        flip = jnp.where(((degree - waves[s]) & 1) == 1, -1.0, 1.0)
        x_v[s, :ROWS] = rows.astype(BF16)
        x_v[s, ROWS:] = (rows * flip).astype(BF16)

    pl.semaphore_wait(barrier, BAND - 1 + GRP - 1)
    for i in range(1, GRP):
        pl.semaphore_signal(plane_sem, inc=1, device_id=(b0, (g0 + i) & (GRP - 1)), device_id_type=MESH)

    scale_in = 1.0 / math.sqrt(N)
    lane = iota((32, 128), 1)
    low = lane < 64
    lane_group = lane >> 5

    def inverse(first, width):
        parts = [(dot(x_v[s], leg_v[s, :, first : first + width]) * scale_in).astype(BF16) for s in range(SLOTS)]
        return sorted_pairs(parts)

    def by_halves(part, h, base, put):
        for blk in range(2):
            at = base + blk * 128
            x = [part[h * 128 + 32 * f : h * 128 + 32 * f + 32, at : at + 128].astype(F32) for f in range(FIELDS)]
            y = [pltpu.roll(v, 64, 1) for v in x]
            for j in range(2):
                put(h * 4 + 2 * blk, j, jnp.where(low, x[2 * j], y[2 * j + 1]))
                put(h * 4 + 2 * blk + 1, j, jnp.where(low, y[2 * j], x[2 * j + 1]))

    x0, y0, z0, c0 = b0 >> 2, b0 & 3, g0 >> 1, g0 & 1

    def peer(t):
        turn = t >> 1
        dx = turn & 3
        dy = ((turn >> 2) + turn) & 3
        dz = ((turn >> 4) + turn) & 3
        b = (((x0 + dx) & 3) << 2) + ((y0 + dy) & 3)
        g = (((z0 + dz) & 3) << 1) + ((c0 + t) & 1)
        return b, g

    def exchange(piece, source, target, which):
        def step(t, carry):
            b, g = peer(t)
            pltpu.make_async_remote_copy(
                src_ref=source(b, g), dst_ref=target, send_sem=ssem.at[which], recv_sem=rsem.at[which],
                device_id=(b, g), device_id_type=MESH,
            ).start()
            return carry

        lax.fori_loop(1, DEV, step, 0)
        own = pltpu.make_async_copy(source(b0, g0), target, own_sem.at[which])
        own.start()
        every = pltpu.make_async_remote_copy(
            src_ref=piece, dst_ref=piece, send_sem=ssem.at[which], recv_sem=rsem.at[which],
            device_id=(b0, g0), device_id_type=MESH,
        )
        return own, every

    def arrived(handle):
        handle[0].wait()
        handle[1].wait_recv()

    others = pl.ds(0, DEV - 1)
    get_a.wait()
    for s, part in enumerate(inverse(0, 256)):

        def put_a(g, j, value, s=s):
            send_a[g, 2 * s + j] = pair_rows(value.astype(BF16))

        for h in range(2):
            by_halves(part, h, 0, put_a)

    pl.semaphore_wait(plane_sem, GRP - 1)
    out_a = exchange(grid_a.at[:, others], lambda b, g: send_a.at[g, :, b], grid_a.at[:, me], 0)

    get_b.wait()
    for s, part in enumerate(inverse(256, 384)):

        def put_b(g, j, value, s=s):
            send_b[g, 3 * s + j] = pair_rows(value.astype(BF16))

        for h in range(2):
            by_halves(part, h, 0, put_b)
            x = [part[h * 128 + 32 * f : h * 128 + 32 * f + 32, 256:384].astype(F32) for f in range(FIELDS)]
            turned = [[v if i == 0 else pltpu.roll(v, 32 * i, 1) for i in range(4)] for v in x]
            for q in range(4):
                put_b(h * 4 + q, 2, pick_group(lane_group, [turned[f][(f - q) % 4] for f in range(FIELDS)]))

    out_b = exchange(grid_b.at[:, others], lambda b, g: send_b.at[g, :, b], grid_b.at[:, me], 1)

    tab = tab_ref[...].reshape(1, M).astype(F32)
    high = jnp.floor(tab * (1.0 / 32))
    rest = tab - 32.0 * high
    row8 = iota((8, M), 0)
    split_rows = jnp.where(row8 == 0, high, jnp.where(row8 == 1, rest, 0.0)).astype(BF16)
    high_rows = jnp.broadcast_to(high, (128, M)).astype(BF16)
    rest_rows = jnp.broadcast_to(rest, (128, M)).astype(BF16)

    def wave_row(s):
        pick = jnp.where(iota((M, 256), 0) == (iota((M, 256), 1) >> 1) * SLOTS + s, 1.0, 0.0).astype(BF16)
        found = dot(split_rows, pick)
        return found[0:1] * 32.0 + found[1:2]

    def wave_column(s):
        pick = jnp.where(iota((256, M), 1) == (iota((256, M), 0) >> 1) * SLOTS + s, 1.0, 0.0).astype(BF16)
        found = 32.0 * lax.dot_general(pick, high_rows, NT, preferred_element_type=F32)
        return found + lax.dot_general(pick, rest_rows, NT, preferred_element_type=F32)

    def is_even(wave):
        return wave - 2.0 * jnp.floor(wave * 0.5) == 0.0

    def split_pair(first, second):
        even = is_even(first)
        return jnp.where(even, first, second), jnp.where(even, second, first)

    def fill_tt(wave, at, odd_at=None):
        quarter = (iota((1, 256), 1) & 1).astype(F32)
        turn = 2.0 * turned_cos(wave * 128.0, 0.0)
        if odd_at is not None:
            even = is_even(wave)

        def strip(i, carry):
            line = (iota((32, 256), 0) + i * 32).astype(F32)
            last = turned_cos(wave * line, quarter)
            value = turned_cos(wave * (line + 128.0), quarter)
            for a in range(HALF // 128):
                rows = pl.ds(pl.multiple_of(a * 128 + i * 32, 32), 32)
                if odd_at is None:
                    tt[rows, at : at + 256] = last.astype(BF16)
                else:
                    tt[rows, at : at + 256] = jnp.where(even, last, 0.0).astype(BF16)
                    tt[rows, odd_at : odd_at + 256] = jnp.where(even, 0.0, last).astype(BF16)
                value, last = turn * value - last, value
            return carry

        lax.fori_loop(0, 4, strip, 0)

    def fill_tr(wave, at):
        for i in range(4):
            w = wave[i * 64 : i * 64 + 64]
            line = iota((64, 128), 1).astype(F32)
            quarter = (iota((64, 128), 0) & 1).astype(F32)
            turn = 2.0 * turned_cos(w * 128.0, 0.0)
            last = turned_cos(w * line, quarter)
            value = turned_cos(w * (line + 128.0), quarter)
            even = is_even(w)
            for a in range(HALF // 128):
                cols = slice(a * 128, a * 128 + 128)
                if at is not None:
                    tr[at + i * 64 : at + i * 64 + 64, cols] = last.astype(BF16)
                else:
                    tr4[i * 64 : i * 64 + 64, cols] = jnp.where(even, last, 0.0).astype(BF16)
                    cols = slice(HALF + a * 128, HALF + a * 128 + 128)
                    tr4[i * 64 : i * 64 + 64, cols] = jnp.where(even, 0.0, last).astype(BF16)
                value, last = turn * value - last, value

    def tables():
        for p in range(2):
            even, odd = split_pair(wave_row(2 * p), wave_row(2 * p + 1))
            fill_tt(even, 256 * p)
            fill_tt(odd, PART + 256 * p)
            even, odd = split_pair(wave_column(2 * p), wave_column(2 * p + 1))
            fill_tr(even, 512 * p)
            fill_tr(odd, 512 * p + 256)
        fill_tt(wave_row(4), 512, PART + 512)
        fill_tr(wave_column(4), None)

    tables()

    scale_zonal = 2.0 / math.sqrt(NLON) / M * 2.0

    def to_grid(grid, prod, blocks):
        def waves_of(parity):
            return jnp.concatenate(
                [
                    jnp.concatenate([flat_rows(grid[s * blocks + j]) for s in (parity, 2 + parity, 4)], axis=0)
                    for j in range(blocks)
                ],
                axis=1,
            )

        even_in, odd_in = waves_of(0), waves_of(1)
        step = 256
        low_lanes = iota((step, 128), 1) < 64

        def chunk(i, carry):
            start = pl.multiple_of(i * step, step)
            even = dot(tt[pl.ds(start, step), :PART], even_in)
            odd = dot(tt[pl.ds(start, step), PART:], odd_in)
            e = [even[:, j * 128 : j * 128 + 128] for j in range(blocks)]
            o = [odd[:, j * 128 : j * 128 + 128] for j in range(blocks)]
            e_next = list(swap_halves(e[0], e[1], low_lanes))
            o_next = list(swap_halves(o[0], o[1], low_lanes))
            if blocks == 3:
                e_next.append(pltpu.roll(e[2], 96, 1))
                o_next.append(pltpu.roll(o[2], 96, 1))
            for j in range(blocks):
                cols = slice(j * 128, j * 128 + 128)
                prod[pl.ds(start, step), cols] = (e[j] * e_next[j] + o[j] * o_next[j]).astype(BF16)
                prod[pl.ds(HALF + start, step), cols] = (e[j] * o_next[j] + o[j] * e_next[j]).astype(BF16)
            return carry

        lax.fori_loop(0, HALF // step, chunk, 0)

    def to_zonal(prod, back, blocks, slots):
        for s in slots:
            if s == 4:
                values = dot(tr4[...], prod[...])
            else:
                half = (s & 1) * HALF
                values = dot(tr[s * 256 : s * 256 + 256, :], prod[half : half + HALF, :])
            values = (values * scale_zonal).astype(BF16)
            for j in range(blocks):
                back[s * blocks + j] = pair_rows(values[:, j * 128 : j * 128 + 128])

    arrived(out_a)
    to_grid(grid_a, prod_a, 2)
    to_zonal(prod_a, back_a, 2, range(SLOTS))
    ret_a = exchange(back_a.at[:, others], lambda b, g: back_a.at[:, b * GRP + g], home_a.at[g0, :, b0], 2)

    arrived(out_b)
    to_grid(grid_b, prod_b, 3)
    returns = []
    for i, (first, end) in enumerate(RETURNS):
        to_zonal(prod_b, back_b, 3, range(first, end))
        span = pl.ds(3 * first, 3 * (end - first))
        returns.append(
            exchange(
                back_b.at[span, others],
                lambda b, g, span=span: back_b.at[span, b * GRP + g],
                home_b.at[g0, span, b0],
                3 + i,
            )
        )

    r = iota((2 * ROWS, 2 * ROWS), 0)
    j = iota((2 * ROWS, 2 * ROWS), 1)
    hit = (j & 127) == ((r & 63) << 1) + ((r >> 6) & 1)
    both_signs = jnp.where(hit, jnp.where((r >= ROWS) & (j >= ROWS), -1.0, 1.0), 0.0).astype(BF16)
    scale_out = 1.0 / math.sqrt(NLAT)

    def from_halves(home, h, row):
        blocks = []
        for blk in range(2):
            z = [[flat_rows(home[h * 4 + 2 * blk + i, row + j]).astype(F32) for j in range(2)] for i in range(2)]
            y = [[pltpu.roll(v, 64, 1) for v in w] for w in z]
            fields = []
            for j in range(2):
                fields.append(jnp.where(low, z[0][j], y[1][j]))
                fields.append(jnp.where(low, y[0][j], z[1][j]))
            blocks.append(jnp.concatenate(fields, axis=0).astype(BF16))
        return blocks

    def gather(s):
        halves = []
        for h in range(2):
            parts = from_halves(home_a, h, 2 * s) + from_halves(home_b, h, 3 * s)
            z = [flat_rows(home_b[h * 4 + q, 3 * s + 2]).astype(F32) for q in range(4)]
            turned = [[v if i == 0 else pltpu.roll(v, 32 * i, 1) for i in range(4)] for v in z]
            mixed = [pick_group(lane_group, [turned[q][(q - f) % 4] for q in range(4)]) for f in range(FIELDS)]
            parts.append(jnp.concatenate(mixed, axis=0).astype(BF16))
            halves.append(jnp.concatenate(parts, axis=1))
        return jnp.concatenate(halves, axis=0)

    def direct(s, rows):
        folded = dot(both_signs, rows).astype(BF16)
        result = lax.dot_general(folded, leg_v[s], NT, preferred_element_type=F32)
        chosen = jnp.where(((degree - waves[s]) & 1) == 0, result[:ROWS], result[ROWS:])
        out_v[s] = jnp.where(degree >= waves[s], chosen * scale_out, 0.0)

    arrived(ret_a)
    for i, (first, end) in enumerate(RETURNS):
        arrived(returns[i])
        rows = [gather(s) for s in range(first, end)]
        if end - first == 2:
            keep = ordered[first // 2]
            rows = [jnp.where(keep, rows[0], rows[1]), jnp.where(keep, rows[1], rows[0])]
        for s in range(first, end):
            direct(s, rows[s - first])
    for handle in [out_a, out_b, ret_a] + returns:
        handle[1].wait_send()


def on_device(spectral, legendre, owner_table):
    anywhere = pl.BlockSpec(memory_space=pl.ANY)
    moves = 3 + len(RETURNS)
    out = pl.pallas_call(
        kernel,
        out_shape=pltpu.VMEM((SLOTS, ROWS, N), F32),
        in_specs=[
            pl.BlockSpec(memory_space=pltpu.SMEM),
            pl.BlockSpec(memory_space=pltpu.VMEM),
            anywhere,
            anywhere,
        ],
        out_specs=pl.BlockSpec(memory_space=pltpu.VMEM),
        scratch_shapes=[
            pltpu.VMEM((SLOTS, ROWS, N), BF16),
            pltpu.VMEM((SLOTS, N, N), BF16),
            pltpu.VMEM((SLOTS, 2 * ROWS, N), BF16),
            pltpu.VMEM((GRP, 2 * SLOTS, LEV, 2, 128), BF16),
            pltpu.VMEM((GRP, 3 * SLOTS, LEV, 2, 128), BF16),
            pltpu.VMEM((2 * SLOTS, DEV, 2, 128), BF16),
            pltpu.VMEM((3 * SLOTS, DEV, 2, 128), BF16),
            pltpu.VMEM((HALF, 2 * PART), BF16),
            pltpu.VMEM((8 * DEV, HALF), BF16),
            pltpu.VMEM((2 * DEV, NLON), BF16),
            pltpu.VMEM((NLON, 256), BF16),
            pltpu.VMEM((NLON, 384), BF16),
            pltpu.VMEM((2 * SLOTS, DEV, 2, 128), BF16),
            pltpu.VMEM((3 * SLOTS, DEV, 2, 128), BF16),
            pltpu.VMEM((GRP, 2 * SLOTS, LEV, 2, 128), BF16),
            pltpu.VMEM((GRP, 3 * SLOTS, LEV, 2, 128), BF16),
            pltpu.SemaphoreType.DMA((3,)),
            pltpu.SemaphoreType.DMA((moves,)),
            pltpu.SemaphoreType.DMA((moves,)),
            pltpu.SemaphoreType.DMA((moves,)),
            pltpu.SemaphoreType.REGULAR,
        ],
        compiler_params=pltpu.CompilerParams(
            collective_id=0, has_side_effects=True, vmem_limit_bytes=61 << 20
        ),
    )(
        owner_table,
        owner_table,
        spectral.reshape(SLOTS, ROWS, N),
        legendre,
    )
    return out.reshape(SLOTS, 2, FIELDS, LEV, N)


def solution(mesh):
    placed = (P(("band", "grp"), None, None, None, None), P(("band", "grp"), None, None), P())
    return jax.shard_map(
        on_device,
        mesh=mesh,
        in_specs=placed,
        out_specs=P(("band", "grp"), None, None, None, None),
        check_vma=False,
    )
```

time: 69.7 us -> 57.1 us (0.82)
  Pallas kernels: 65.5 us -> 55.8 us
  local copies, waits for them, and re-layouts: 4 us -> 1.17 us
    pallas_call x1, Pallas kernels: 65.5 us -> 55.8 us  [on_device(): pl.pallas_call(kernel, out_shape=pltpu.VMEM((SLOTS, ROWS, N), F32), in_sp...]
    unnamed x1, local copies, waits for them, and re-layouts: 2.73 us -> 1.17 us
    reshape x1 -> x0, local copies, waits for them, and re-layouts: 1.27 us -> none  [on_device(): owner_table.reshape(1, M)]
where the time goes in v2:
time: 57.1 us; the launch traced here: 57 us
  Pallas kernels  55.8 us (98%)
  local copies, waits for them, and re-layouts  1.17 us (2%)
    pallas_call x1, Pallas kernels, on_device(): pl.pallas_call(kernel, out_shape=pltpu.VMEM((SLOTS, ROWS, N), F32), in_sp...  55.8 us
    unnamed x1, local copies, waits for them, and re-layouts  1.17 us

profile of v2, /device:TPU:1, one launch (start us, length us, event | category | flops | bytes accessed | tf_op | source)
XLA Modules:
  0.0 57.0 jit_solution(13290027251389428187)
XLA Ops:
  0.0 55.8 %shard_map.37 = f32[5,128,640]{2,1,0:T(8,128)S(1)} custom-call(s32[640]{0:T(1024)} %tab_ref.1, s32[640]{0:T(1024)} %tab_ref.1, bf16[5,128,640]{2,1,0:T(8,128)(2,1)} %bitcast.3, bf16[5,640,640]{2,1,0:T(8,128)(2,1)} %leg_hbm.1), custom_call_target="tpu_custom_call" | custom-call | tf_op jit(solution)/shard_map/pallas_call | solution.py:397
  55.8 1.2 %copy.5 = f32[5,2,4,16,640]{4,3,2,1,0:T(8,128)} copy(f32[5,2,4,16,640]{4,3,2,1,0:T(8,128)S(1)} %bitcast.2) | data formatting | bytes 3276800

commit v3 on v2

--- a/solution.py
+++ b/solution.py
@@ -36,17 +36,15 @@
     return lax.broadcasted_iota(jnp.int32, shape, axis)
 
 
-def turned_cos(turns, quarter):
-    whole = jnp.floor(turns * (4.0 / NLON) + 0.5)
-    x = (turns - whole * (NLON / 4.0)) * (2.0 * math.pi / NLON)
+def turned_cos(turns):
+    near = turns - jnp.floor(turns * (1.0 / NLON) + 0.5) * NLON
+    x = near * (math.pi / NLON)
     y = x * x
-    cosine = 1.0 + y * (-0.5 + y * (1.0 / 24 + y * (-1.0 / 720 + y * (1.0 / 40320))))
-    sine = x * (1.0 + y * (-1.0 / 6 + y * (1.0 / 120 + y * (-1.0 / 5040 + y * (1.0 / 362880)))))
-    k = whole + quarter
-    k = k - 4.0 * jnp.floor(k * 0.25)
-    odd = (k == 1.0) | (k == 3.0)
-    value = jnp.where(odd, sine, cosine)
-    return jnp.where((k == 1.0) | (k == 2.0), -value, value)
+    sine = 1.0 / 6227020800
+    for n in (11, 9, 7, 5, 3, 1):
+        sine = (-1.0 if n % 4 == 3 else 1.0) / math.factorial(n) + y * sine
+    sine = x * sine
+    return 1.0 - 2.0 * (sine * sine)
 
 
 def pair_rows(x):
@@ -72,27 +70,28 @@
 
 def kernel(
     tab_smem, tab_ref, spec_hbm, leg_hbm, out_v,
-    spec_v, leg_v, x_v, send_a, send_b, grid_a, grid_b, tt, tr, tr4, prod_a, prod_b,
-    back_a, back_b, home_a, home_b,
+    spec_v, leg_v, x_v, send_a, send_q, send_b, grid_a, grid_q, grid_b, tt, tr, tr4, prod_a, prod_q, prod_b,
+    back_a, back_q, back_b, home_a, home_q, home_b,
     in_sem, own_sem, ssem, rsem, plane_sem,
 ):
     b0 = lax.axis_index("band")
     g0 = lax.axis_index("grp")
     me = b0 * GRP + g0
 
+    parts = [(0, 256), (256, 128), (384, 256)]
+    get_spec = pltpu.make_async_copy(spec_hbm, spec_v, in_sem.at[0])
+    get_spec.start()
+    get_leg = []
+    for i, (first, width) in enumerate(parts):
+        cols = pl.ds(first, width)
+        get_leg.append(pltpu.make_async_copy(leg_hbm.at[:, :, cols], leg_v.at[:, :, cols], in_sem.at[1 + i]))
+        get_leg[-1].start()
+
     barrier = pltpu.get_barrier_semaphore()
     for i in range(1, BAND):
         pl.semaphore_signal(barrier, inc=1, device_id=((b0 + i) & (BAND - 1), g0), device_id_type=MESH)
     for i in range(1, GRP):
         pl.semaphore_signal(barrier, inc=1, device_id=(b0, (g0 + i) & (GRP - 1)), device_id_type=MESH)
-
-    cols_a, cols_b = pl.ds(0, 256), pl.ds(256, 384)
-    get_spec = pltpu.make_async_copy(spec_hbm, spec_v, in_sem.at[0])
-    get_a = pltpu.make_async_copy(leg_hbm.at[:, :, cols_a], leg_v.at[:, :, cols_a], in_sem.at[1])
-    get_b = pltpu.make_async_copy(leg_hbm.at[:, :, cols_b], leg_v.at[:, :, cols_b], in_sem.at[2])
-    get_spec.start()
-    get_a.start()
-    get_b.start()
 
     degree = iota((1, N), 1)
     waves = [tab_smem[me * SLOTS + s] for s in range(SLOTS)]
@@ -128,9 +127,9 @@
         parts = [(dot(x_v[s], leg_v[s, :, first : first + width]) * scale_in).astype(BF16) for s in range(SLOTS)]
         return sorted_pairs(parts)
 
-    def by_halves(part, h, base, put):
+    def by_halves(part, h, put):
         for blk in range(2):
-            at = base + blk * 128
+            at = blk * 128
             x = [part[h * 128 + 32 * f : h * 128 + 32 * f + 32, at : at + 128].astype(F32) for f in range(FIELDS)]
             y = [pltpu.roll(v, 64, 1) for v in x]
             for j in range(2):
@@ -139,25 +138,20 @@
 
     x0, y0, z0, c0 = b0 >> 2, b0 & 3, g0 >> 1, g0 & 1
 
-    def peer(t):
-        turn = t >> 1
-        dx = turn & 3
-        dy = ((turn >> 2) + turn) & 3
-        dz = ((turn >> 4) + turn) & 3
-        b = (((x0 + dx) & 3) << 2) + ((y0 + dy) & 3)
-        g = (((z0 + dz) & 3) << 1) + ((c0 + t) & 1)
-        return b, g
-
     def exchange(piece, source, target, which):
-        def step(t, carry):
-            b, g = peer(t)
-            pltpu.make_async_remote_copy(
-                src_ref=source(b, g), dst_ref=target, send_sem=ssem.at[which], recv_sem=rsem.at[which],
-                device_id=(b, g), device_id_type=MESH,
-            ).start()
+        def step(i, carry, first=0):
+            for t in range(first, 8):
+                j = t >> 1
+                b = (((x0 + j) & 3) << 2) + ((y0 + i + j) & 3)
+                g = (((z0 + (i >> 2) + j) & 3) << 1) + (c0 ^ (t & 1))
+                pltpu.make_async_remote_copy(
+                    src_ref=source(b, g), dst_ref=target, send_sem=ssem.at[which], recv_sem=rsem.at[which],
+                    device_id=(b, g), device_id_type=MESH,
+                ).start()
             return carry
 
-        lax.fori_loop(1, DEV, step, 0)
+        step(0, 0, 1)
+        lax.fori_loop(1, DEV // 8, step, 0)
         own = pltpu.make_async_copy(source(b0, g0), target, own_sem.at[which])
         own.start()
         every = pltpu.make_async_remote_copy(
@@ -171,32 +165,33 @@
         handle[1].wait_recv()
 
     others = pl.ds(0, DEV - 1)
-    get_a.wait()
-    for s, part in enumerate(inverse(0, 256)):
-
-        def put_a(g, j, value, s=s):
-            send_a[g, 2 * s + j] = pair_rows(value.astype(BF16))
-
-        for h in range(2):
-            by_halves(part, h, 0, put_a)
-
+
+    def halves_out(which, send):
+        get_leg[which].wait()
+        for s, part in enumerate(inverse(*parts[which])):
+
+            def put(g, j, value, s=s):
+                send[g, 2 * s + j] = pair_rows(value.astype(BF16))
+
+            for h in range(2):
+                by_halves(part, h, put)
+
+    halves_out(0, send_a)
     pl.semaphore_wait(plane_sem, GRP - 1)
     out_a = exchange(grid_a.at[:, others], lambda b, g: send_a.at[g, :, b], grid_a.at[:, me], 0)
 
-    get_b.wait()
-    for s, part in enumerate(inverse(256, 384)):
-
-        def put_b(g, j, value, s=s):
-            send_b[g, 3 * s + j] = pair_rows(value.astype(BF16))
-
+    get_leg[1].wait()
+    for s, part in enumerate(inverse(*parts[1])):
         for h in range(2):
-            by_halves(part, h, 0, put_b)
-            x = [part[h * 128 + 32 * f : h * 128 + 32 * f + 32, 256:384].astype(F32) for f in range(FIELDS)]
+            x = [part[h * 128 + 32 * f : h * 128 + 32 * f + 32].astype(F32) for f in range(FIELDS)]
             turned = [[v if i == 0 else pltpu.roll(v, 32 * i, 1) for i in range(4)] for v in x]
             for q in range(4):
-                put_b(h * 4 + q, 2, pick_group(lane_group, [turned[f][(f - q) % 4] for f in range(FIELDS)]))
-
-    out_b = exchange(grid_b.at[:, others], lambda b, g: send_b.at[g, :, b], grid_b.at[:, me], 1)
+                value = pick_group(lane_group, [turned[f][(f - q) % 4] for f in range(FIELDS)])
+                send_q[h * 4 + q, s] = pair_rows(value.astype(BF16))
+    out_q = exchange(grid_q.at[:, others], lambda b, g: send_q.at[g, :, b], grid_q.at[:, me], 1)
+
+    halves_out(2, send_b)
+    out_b = exchange(grid_b.at[:, others], lambda b, g: send_b.at[g, :, b], grid_b.at[:, me], 2)
 
     tab = tab_ref[...].reshape(1, M).astype(F32)
     high = jnp.floor(tab * (1.0 / 32))
@@ -224,17 +219,18 @@
         return jnp.where(even, first, second), jnp.where(even, second, first)
 
     def fill_tt(wave, at, odd_at=None):
-        quarter = (iota((1, 256), 1) & 1).astype(F32)
-        turn = 2.0 * turned_cos(wave * 128.0, 0.0)
+        quarter = ((iota((1, 256), 1) & 1) * (NLON // 4)).astype(F32)
+        turn = 2.0 * turned_cos(wave * 64.0)
         if odd_at is not None:
             even = is_even(wave)
 
         def strip(i, carry):
             line = (iota((32, 256), 0) + i * 32).astype(F32)
-            last = turned_cos(wave * line, quarter)
-            value = turned_cos(wave * (line + 128.0), quarter)
-            for a in range(HALF // 128):
-                rows = pl.ds(pl.multiple_of(a * 128 + i * 32, 32), 32)
+            turns = wave * line + quarter
+            last = turned_cos(turns)
+            value = turned_cos(turns + wave * 64.0)
+            for a in range(HALF // 64):
+                rows = pl.ds(pl.multiple_of(a * 64 + i * 32, 32), 32)
                 if odd_at is None:
                     tt[rows, at : at + 256] = last.astype(BF16)
                 else:
@@ -243,16 +239,18 @@
                 value, last = turn * value - last, value
             return carry
 
-        lax.fori_loop(0, 4, strip, 0)
+        lax.fori_loop(0, 2, strip, 0)
 
     def fill_tr(wave, at):
         for i in range(4):
             w = wave[i * 64 : i * 64 + 64]
             line = iota((64, 128), 1).astype(F32)
-            quarter = (iota((64, 128), 0) & 1).astype(F32)
-            turn = 2.0 * turned_cos(w * 128.0, 0.0)
-            last = turned_cos(w * line, quarter)
-            value = turned_cos(w * (line + 128.0), quarter)
+            quarter = ((iota((64, 128), 0) & 1) * (NLON // 4)).astype(F32)
+            step = w * 128.0
+            turn = 2.0 * turned_cos(step)
+            turns = w * line + quarter
+            last = turned_cos(turns)
+            value = turned_cos(turns + step)
             even = is_even(w)
             for a in range(HALF // 128):
                 cols = slice(a * 128, a * 128 + 128)
@@ -299,11 +297,12 @@
             odd = dot(tt[pl.ds(start, step), PART:], odd_in)
             e = [even[:, j * 128 : j * 128 + 128] for j in range(blocks)]
             o = [odd[:, j * 128 : j * 128 + 128] for j in range(blocks)]
-            e_next = list(swap_halves(e[0], e[1], low_lanes))
-            o_next = list(swap_halves(o[0], o[1], low_lanes))
-            if blocks == 3:
-                e_next.append(pltpu.roll(e[2], 96, 1))
-                o_next.append(pltpu.roll(o[2], 96, 1))
+            if blocks == 2:
+                e_next = swap_halves(e[0], e[1], low_lanes)
+                o_next = swap_halves(o[0], o[1], low_lanes)
+            else:
+                e_next = [pltpu.roll(e[0], 96, 1)]
+                o_next = [pltpu.roll(o[0], 96, 1)]
             for j in range(blocks):
                 cols = slice(j * 128, j * 128 + 128)
                 prod[pl.ds(start, step), cols] = (e[j] * e_next[j] + o[j] * o_next[j]).astype(BF16)
@@ -326,20 +325,25 @@
     arrived(out_a)
     to_grid(grid_a, prod_a, 2)
     to_zonal(prod_a, back_a, 2, range(SLOTS))
-    ret_a = exchange(back_a.at[:, others], lambda b, g: back_a.at[:, b * GRP + g], home_a.at[g0, :, b0], 2)
+    ret_a = exchange(back_a.at[:, others], lambda b, g: back_a.at[:, b * GRP + g], home_a.at[g0, :, b0], 3)
+
+    arrived(out_q)
+    to_grid(grid_q, prod_q, 1)
+    to_zonal(prod_q, back_q, 1, range(SLOTS))
+    ret_q = exchange(back_q.at[:, others], lambda b, g: back_q.at[:, b * GRP + g], home_q.at[g0, :, b0], 4)
 
     arrived(out_b)
-    to_grid(grid_b, prod_b, 3)
+    to_grid(grid_b, prod_b, 2)
     returns = []
     for i, (first, end) in enumerate(RETURNS):
-        to_zonal(prod_b, back_b, 3, range(first, end))
-        span = pl.ds(3 * first, 3 * (end - first))
+        to_zonal(prod_b, back_b, 2, range(first, end))
+        span = pl.ds(2 * first, 2 * (end - first))
         returns.append(
             exchange(
                 back_b.at[span, others],
                 lambda b, g, span=span: back_b.at[span, b * GRP + g],
                 home_b.at[g0, span, b0],
-                3 + i,
+                5 + i,
             )
         )
 
@@ -364,12 +368,11 @@
     def gather(s):
         halves = []
         for h in range(2):
-            parts = from_halves(home_a, h, 2 * s) + from_halves(home_b, h, 3 * s)
-            z = [flat_rows(home_b[h * 4 + q, 3 * s + 2]).astype(F32) for q in range(4)]
+            z = [flat_rows(home_q[h * 4 + q, s]).astype(F32) for q in range(4)]
             turned = [[v if i == 0 else pltpu.roll(v, 32 * i, 1) for i in range(4)] for v in z]
             mixed = [pick_group(lane_group, [turned[q][(q - f) % 4] for q in range(4)]) for f in range(FIELDS)]
-            parts.append(jnp.concatenate(mixed, axis=0).astype(BF16))
-            halves.append(jnp.concatenate(parts, axis=1))
+            middle = [jnp.concatenate(mixed, axis=0).astype(BF16)]
+            halves.append(jnp.concatenate(from_halves(home_a, h, 2 * s) + middle + from_halves(home_b, h, 2 * s), axis=1))
         return jnp.concatenate(halves, axis=0)
 
     def direct(s, rows):
@@ -379,6 +382,7 @@
         out_v[s] = jnp.where(degree >= waves[s], chosen * scale_out, 0.0)
 
     arrived(ret_a)
+    arrived(ret_q)
     for i, (first, end) in enumerate(RETURNS):
         arrived(returns[i])
         rows = [gather(s) for s in range(first, end)]
@@ -387,13 +391,13 @@
             rows = [jnp.where(keep, rows[0], rows[1]), jnp.where(keep, rows[1], rows[0])]
         for s in range(first, end):
             direct(s, rows[s - first])
-    for handle in [out_a, out_b, ret_a] + returns:
+    for handle in [out_a, out_q, out_b, ret_a, ret_q] + returns:
         handle[1].wait_send()
 
 
 def on_device(spectral, legendre, owner_table):
     anywhere = pl.BlockSpec(memory_space=pl.ANY)
-    moves = 3 + len(RETURNS)
+    moves = 5 + len(RETURNS)
     out = pl.pallas_call(
         kernel,
         out_shape=pltpu.VMEM((SLOTS, ROWS, N), F32),
@@ -408,20 +412,15 @@
             pltpu.VMEM((SLOTS, ROWS, N), BF16),
             pltpu.VMEM((SLOTS, N, N), BF16),
             pltpu.VMEM((SLOTS, 2 * ROWS, N), BF16),
-            pltpu.VMEM((GRP, 2 * SLOTS, LEV, 2, 128), BF16),
-            pltpu.VMEM((GRP, 3 * SLOTS, LEV, 2, 128), BF16),
-            pltpu.VMEM((2 * SLOTS, DEV, 2, 128), BF16),
-            pltpu.VMEM((3 * SLOTS, DEV, 2, 128), BF16),
+            *[pltpu.VMEM((GRP, n * SLOTS, LEV, 2, 128), BF16) for n in (2, 1, 2)],
+            *[pltpu.VMEM((n * SLOTS, DEV, 2, 128), BF16) for n in (2, 1, 2)],
             pltpu.VMEM((HALF, 2 * PART), BF16),
             pltpu.VMEM((8 * DEV, HALF), BF16),
             pltpu.VMEM((2 * DEV, NLON), BF16),
-            pltpu.VMEM((NLON, 256), BF16),
-            pltpu.VMEM((NLON, 384), BF16),
-            pltpu.VMEM((2 * SLOTS, DEV, 2, 128), BF16),
-            pltpu.VMEM((3 * SLOTS, DEV, 2, 128), BF16),
-            pltpu.VMEM((GRP, 2 * SLOTS, LEV, 2, 128), BF16),
-            pltpu.VMEM((GRP, 3 * SLOTS, LEV, 2, 128), BF16),
-            pltpu.SemaphoreType.DMA((3,)),
+            *[pltpu.VMEM((NLON, n * 128), BF16) for n in (2, 1, 2)],
+            *[pltpu.VMEM((n * SLOTS, DEV, 2, 128), BF16) for n in (2, 1, 2)],
+            *[pltpu.VMEM((GRP, n * SLOTS, LEV, 2, 128), BF16) for n in (2, 1, 2)],
+            pltpu.SemaphoreType.DMA((4,)),
             pltpu.SemaphoreType.DMA((moves,)),
             pltpu.SemaphoreType.DMA((moves,)),
             pltpu.SemaphoreType.DMA((moves,)),

time: 57.1 us -> 53.4 us (0.935)
  Pallas kernels: 55.8 us -> 52.1 us
    pallas_call x1, Pallas kernels: 55.8 us -> 52.1 us  [on_device(): pl.pallas_call(kernel, out_shape=pltpu.VMEM((SLOTS, ROWS, N), F32), in_sp...]
where the time goes in v3:
time: 53.4 us; the launch traced here: 53.3 us
  Pallas kernels  52.1 us (98%)
  local copies, waits for them, and re-layouts  1.17 us (2%)
    pallas_call x1, Pallas kernels, on_device(): pl.pallas_call(kernel, out_shape=pltpu.VMEM((SLOTS, ROWS, N), F32), in_sp...  52.1 us
    unnamed x1, local copies, waits for them, and re-layouts  1.17 us

profile of v3, /device:TPU:1, one launch (start us, length us, event | category | flops | bytes accessed | tf_op | source)
XLA Modules:
  0.0 53.3 jit_solution(15427221384810757715)
XLA Ops:
  0.0 52.1 %shard_map.37 = f32[5,128,640]{2,1,0:T(8,128)S(1)} custom-call(s32[640]{0:T(1024)} %tab_ref.1, s32[640]{0:T(1024)} %tab_ref.1, bf16[5,128,640]{2,1,0:T(8,128)(2,1)} %bitcast.3, bf16[5,640,640]{2,1,0:T(8,128)(2,1)} %leg_hbm.1), custom_call_target="tpu_custom_call" | custom-call | tf_op jit(solution)/shard_map/pallas_call | solution.py:401
  52.1 1.2 %copy.5 = f32[5,2,4,16,640]{4,3,2,1,0:T(8,128)} copy(f32[5,2,4,16,640]{4,3,2,1,0:T(8,128)S(1)} %bitcast.2) | data formatting | bytes 3276800

commit v4 on v3

--- a/solution.py
+++ b/solution.py
@@ -141,9 +141,9 @@
     def exchange(piece, source, target, which):
         def step(i, carry, first=0):
             for t in range(first, 8):
-                j = t >> 1
+                j = (0, 1, 3, 2)[t >> 1]
                 b = (((x0 + j) & 3) << 2) + ((y0 + i + j) & 3)
-                g = (((z0 + (i >> 2) + j) & 3) << 1) + (c0 ^ (t & 1))
+                g = (((z0 + (i >> 2) + i - j) & 3) << 1) + (c0 ^ (t & 1))
                 pltpu.make_async_remote_copy(
                     src_ref=source(b, g), dst_ref=target, send_sem=ssem.at[which], recv_sem=rsem.at[which],
                     device_id=(b, g), device_id_type=MESH,

time: 53.4 us -> 53.2 us (level)
  no operation moved by 1% of the time
where the time goes in v4:
time: 53.2 us; the launch traced here: 53.1 us
  Pallas kernels  51.9 us (98%)
  local copies, waits for them, and re-layouts  1.17 us (2%)
    pallas_call x1, Pallas kernels, on_device(): pl.pallas_call(kernel, out_shape=pltpu.VMEM((SLOTS, ROWS, N), F32), in_sp...  51.9 us
    unnamed x1, local copies, waits for them, and re-layouts  1.17 us

profile of v4, /device:TPU:1, one launch (start us, length us, event | category | flops | bytes accessed | tf_op | source)
XLA Modules:
  0.0 53.1 jit_solution(14345258112935516142)
XLA Ops:
  0.0 51.9 %shard_map.37 = f32[5,128,640]{2,1,0:T(8,128)S(1)} custom-call(s32[640]{0:T(1024)} %tab_ref.1, s32[640]{0:T(1024)} %tab_ref.1, bf16[5,128,640]{2,1,0:T(8,128)(2,1)} %bitcast.3, bf16[5,640,640]{2,1,0:T(8,128)(2,1)} %leg_hbm.1), custom_call_target="tpu_custom_call" | custom-call | tf_op jit(solution)/shard_map/pallas_call | solution.py:401
  51.9 1.2 %copy.5 = f32[5,2,4,16,640]{4,3,2,1,0:T(8,128)} copy(f32[5,2,4,16,640]{4,3,2,1,0:T(8,128)S(1)} %bitcast.2) | data formatting | bytes 3276800
